TPU v7x, 32 devices: a whole 2x2x4 slice. The times are simulated.
32 devices in a mesh: shard: 8 (over y, x, core), rep: 4 (over z).
Axes of the slice: x: 2, y: 2, z: 4, core: 2. Of those that a mesh axis runs over, the one named last changes fastest.
Arguments:
- tokens: bfloat16 [2, 16384, 768], P(None, ('shard', 'rep')), may hold values from -6 to 6
- segment_ids: int32 [2, 16384], P(None, ('shard', 'rep')), may hold values from 0 to 7, as said below
- qkv_weight: bfloat16 [768, 2304], P('shard'), may hold values from -0.21875 to 0.21875
- out_weight: bfloat16 [768, 768], P('shard'), may hold values from -0.875 to 0.875
- gate_weight: bfloat16 [768, 3072], P('shard'), may hold values from -0.21875 to 0.21875
- up_weight: bfloat16 [768, 3072], P('shard'), may hold values from -0.21875 to 0.21875
- down_weight: bfloat16 [3072, 768], P('shard'), may hold values from -0.109375 to 0.109375
- norm1_gain: bfloat16 [768], P('shard'), may hold values from 0.5 to 1.5
- norm1_bias: bfloat16 [768], P('shard'), may hold values from -1 to 1
- norm2_gain: bfloat16 [768], P('shard'), may hold values from 0.5 to 1.5
- norm2_bias: bfloat16 [768], P('shard'), may hold values from -1 to 1
- out_grad: bfloat16 [2, 16384, 768], P(None, ('shard', 'rep')), may hold values from -6 to 6
Outputs:
- output: bfloat16 [2, 16384, 768], P(None, ('shard', 'rep'))
- input_grad: bfloat16 [2, 16384, 768], P(None, ('shard', 'rep'))
- qkv_weight_grad: float32 [768, 2304], P('shard')
- out_weight_grad: float32 [768, 768], P('shard')
- gate_weight_grad: float32 [768, 3072], P('shard')
- up_weight_grad: float32 [768, 3072], P('shard')
- down_weight_grad: float32 [3072, 768], P('shard')
- norm1_gain_grad: float32 [768], P('shard')
- norm1_bias_grad: float32 [768], P('shard')
- norm2_gain_grad: float32 [768], P('shard')
- norm2_bias_grad: float32 [768], P('shard')
Inputs may be any that keep to these rules, and one draw needn't show every extreme that they name: Within each packed sequence of 512 tokens segment_ids never falls, starts at 0, and takes each value 0 to 7 on a run of one or more tokens.
All inputs are finite; a program needn't handle non-finite values.
Results may differ from a plain program's by a relative error of at most 0.02.
Values may be sent and summed in bfloat16 or wider, within the bound.
No kernel may reach another device: no remote copies, remote signals or barrier semaphores. Data moves between devices by JAX's collectives and lax.ppermute only.
A program may use at most 192 MiB of HBM per device.

v0:
```python
import jax
import jax.numpy as jnp
from jax import lax
from jax.sharding import PartitionSpec as P

HEAD_DIM = 64
norm_eps = 1e-12
rope_base = 1000.0
masked_score = -1000000000.0


def matmul(left_op, right_op):
    return jnp.dot(left_op, right_op, preferred_element_type=jnp.float32)


def inner_sum(left_op, right_op):
    return lax.dot_general(
        left_op, right_op, (((0,), (0,)), ((), ())), preferred_element_type=jnp.float32
    )


def times_transposed(left_op, right_op):
    return lax.dot_general(
        left_op, right_op, (((1,), (1,)), ((), ())), preferred_element_type=jnp.float32
    )


def rope_tables(seq_len, head_dim):
    places = jnp.arange(seq_len, dtype=jnp.int32).astype(jnp.float32)
    frequency = rope_base ** (-jnp.arange(0, head_dim, 2, dtype=jnp.float32) / head_dim)
    angles = places[:, None] * frequency[None, :]
    cos_table = jnp.cos(angles)
    sin_table = jnp.sin(angles)
    return (
        jnp.concatenate([cos_table, cos_table], -1),
        jnp.concatenate([sin_table, sin_table], -1),
    )


def rotate(values, cos_table, sin_table):
    half_dim = values.shape[-1] // 2
    turned = jnp.concatenate([-values[..., half_dim:], values[..., :half_dim]], -1)
    return values * cos_table + turned * sin_table


def rotate_back(grad_in, cos_table, sin_table):
    half_dim = grad_in.shape[-1] // 2
    scaled = grad_in * sin_table
    turned = jnp.concatenate([scaled[..., half_dim:], -scaled[..., :half_dim]], -1)
    return grad_in * cos_table + turned


def normalize(hidden_in):
    centre = hidden_in - jnp.mean(hidden_in, -1, keepdims=True)
    inv_std = lax.rsqrt(jnp.mean(centre * centre, -1, keepdims=True) + norm_eps)
    return (centre * inv_std, inv_std)


def norm_back(grad_norm, normed, inv_std):
    return inv_std * (
        grad_norm
        - jnp.mean(grad_norm, -1, keepdims=True)
        - normed * jnp.mean(grad_norm * normed, -1, keepdims=True)
    )


def attend_head(query_h, key_h, value_h, same_doc):
    scores = jnp.where(same_doc, times_transposed(query_h, key_h) * 0.125, masked_score)
    row_max = jnp.max(scores, -1, keepdims=True)
    expo = jnp.exp(scores - row_max)
    total_sum = jnp.sum(expo, -1, keepdims=True)
    probs = expo / total_sum
    result = matmul(probs.astype(jnp.bfloat16), value_h)
    return (result, (row_max + jnp.log(total_sum))[:, 0])


def head_backward(query_h, key_h, value_h, grad_h, log_total, same_doc):
    scores = jnp.where(same_doc, times_transposed(query_h, key_h) * 0.125, masked_score)
    probs = jnp.exp(scores - log_total[:, None])
    grad_value = inner_sum(probs.astype(jnp.bfloat16), grad_h)
    grad_probs = times_transposed(grad_h, value_h)
    grad_scores = (probs * (grad_probs - jnp.sum(probs * grad_probs, -1, keepdims=True))).astype(
        jnp.bfloat16
    )
    grad_query = matmul(grad_scores, key_h) * 0.125
    grad_key = inner_sum(grad_scores, query_h) * 0.125
    return (grad_query, grad_key, grad_value)


def forward_pass(token_rows, segment, weight_set):
    full_qkv, full_out, full_gate, full_up, full_down, gain_one, bias_one, gain_two, bias_two = (
        weight_set
    )
    seq_len = token_rows.shape[0]
    width = full_out.shape[0]
    head_count = width // HEAD_DIM
    cos_table, sin_table = rope_tables(seq_len, HEAD_DIM)
    cos_heads = cos_table[:, None, :]
    sin_heads = sin_table[:, None, :]
    joint = matmul(token_rows, full_qkv)
    queries = (
        rotate(joint[:, :width].reshape(seq_len, head_count, HEAD_DIM), cos_heads, sin_heads)
        .astype(jnp.bfloat16)
        .transpose(1, 0, 2)
    )
    key_rows = (
        rotate(
            joint[:, width : 2 * width].reshape(seq_len, head_count, HEAD_DIM), cos_heads, sin_heads
        )
        .astype(jnp.bfloat16)
        .transpose(1, 0, 2)
    )
    value_rows = (
        joint[:, 2 * width :]
        .reshape(seq_len, head_count, HEAD_DIM)
        .astype(jnp.bfloat16)
        .transpose(1, 0, 2)
    )
    same_doc = segment[:, None] == segment[None, :]
    attended, log_total = lax.map(
        lambda operands: attend_head(operands[0], operands[1], operands[2], same_doc),
        (queries, key_rows, value_rows),
    )
    attended_low = attended.transpose(1, 0, 2).reshape(seq_len, width).astype(jnp.bfloat16)
    residual_one = token_rows.astype(jnp.float32) + matmul(attended_low, full_out)
    normed_one, inv_one = normalize(residual_one)
    mixed = normed_one * gain_one.astype(jnp.float32) + bias_one.astype(jnp.float32)
    mixed_low = mixed.astype(jnp.bfloat16)
    gate_pre = matmul(mixed_low, full_gate)
    up_pre = matmul(mixed_low, full_up)
    sigmoid_gate = jax.nn.sigmoid(gate_pre)
    hidden_low = (gate_pre * sigmoid_gate * up_pre).astype(jnp.bfloat16)
    residual_two = mixed + matmul(hidden_low, full_down)
    normed_two, inv_two = normalize(residual_two)
    layer_out = (normed_two * gain_two.astype(jnp.float32) + bias_two.astype(jnp.float32)).astype(
        jnp.bfloat16
    )
    kept = {
        "token_rows": token_rows,
        "cos_heads": cos_heads,
        "sin_heads": sin_heads,
        "queries": queries,
        "key_rows": key_rows,
        "value_rows": value_rows,
        "log_total": log_total,
        "same_doc": same_doc,
        "attended_low": attended_low,
        "normed_one": normed_one,
        "inv_one": inv_one,
        "mixed_low": mixed_low,
        "gate_pre": gate_pre,
        "up_pre": up_pre,
        "sigmoid_gate": sigmoid_gate,
        "hidden_low": hidden_low,
        "normed_two": normed_two,
        "inv_two": inv_two,
    }
    return (kept, layer_out)


def backward_pass(kept, weight_set, cotangent):
    full_qkv, full_out, full_gate, full_up, full_down, gain_one, gain_two = weight_set
    token_rows = kept["token_rows"]
    seq_len = token_rows.shape[0]
    width = full_out.shape[0]
    head_count = width // HEAD_DIM
    grad_gain_two = jnp.sum(cotangent * kept["normed_two"], 0)
    grad_bias_two = jnp.sum(cotangent, 0)
    grad_res_two = norm_back(
        cotangent * gain_two.astype(jnp.float32), kept["normed_two"], kept["inv_two"]
    )
    grad_mlp = grad_res_two.astype(jnp.bfloat16)
    grad_down = inner_sum(kept["hidden_low"], grad_mlp)
    grad_hidden = times_transposed(grad_mlp, full_down)
    gate_pre = kept["gate_pre"]
    sigmoid_gate = kept["sigmoid_gate"]
    grad_up_pre = (grad_hidden * gate_pre * sigmoid_gate).astype(jnp.bfloat16)
    grad_gate_pre = (
        grad_hidden * kept["up_pre"] * sigmoid_gate * (1.0 + gate_pre * (1.0 - sigmoid_gate))
    ).astype(jnp.bfloat16)
    grad_gate = inner_sum(kept["mixed_low"], grad_gate_pre)
    grad_up = inner_sum(kept["mixed_low"], grad_up_pre)
    grad_mixed = (
        grad_res_two
        + times_transposed(grad_gate_pre, full_gate)
        + times_transposed(grad_up_pre, full_up)
    )
    grad_gain_one = jnp.sum(grad_mixed * kept["normed_one"], 0)
    grad_bias_one = jnp.sum(grad_mixed, 0)
    grad_res_one = norm_back(
        grad_mixed * gain_one.astype(jnp.float32), kept["normed_one"], kept["inv_one"]
    )
    grad_branch = grad_res_one.astype(jnp.bfloat16)
    grad_out = inner_sum(kept["attended_low"], grad_branch)
    grad_att = (
        times_transposed(grad_branch, full_out)
        .astype(jnp.bfloat16)
        .reshape(seq_len, head_count, HEAD_DIM)
        .transpose(1, 0, 2)
    )
    same_doc = kept["same_doc"]
    grad_query, grad_key, grad_value = lax.map(
        lambda operands: head_backward(
            operands[0], operands[1], operands[2], operands[3], operands[4], same_doc
        ),
        (kept["queries"], kept["key_rows"], kept["value_rows"], grad_att, kept["log_total"]),
    )
    query_part = rotate_back(
        grad_query.transpose(1, 0, 2), kept["cos_heads"], kept["sin_heads"]
    ).reshape(seq_len, width)
    key_part = rotate_back(
        grad_key.transpose(1, 0, 2), kept["cos_heads"], kept["sin_heads"]
    ).reshape(seq_len, width)
    value_part = grad_value.transpose(1, 0, 2).reshape(seq_len, width)
    grad_joint = jnp.concatenate([query_part, key_part, value_part], -1).astype(jnp.bfloat16)
    grad_qkv = inner_sum(token_rows, grad_joint)
    input_grad = (grad_res_one + times_transposed(grad_joint, full_qkv)).astype(jnp.bfloat16)
    return (
        (
            grad_qkv,
            grad_out,
            grad_gate,
            grad_up,
            grad_down,
            grad_gain_one,
            grad_bias_one,
            grad_gain_two,
            grad_bias_two,
        ),
        input_grad,
    )


def shards(
    tokens,
    segment_ids,
    qkv_weight,
    out_weight,
    gate_weight,
    up_weight,
    down_weight,
    norm1_gain,
    norm1_bias,
    norm2_gain,
    norm2_bias,
    out_grad,
):
    owned_shards = (
        qkv_weight,
        out_weight,
        gate_weight,
        up_weight,
        down_weight,
        norm1_gain,
        norm1_bias,
        norm2_gain,
        norm2_bias,
    )
    group_count = lax.axis_size("shard")
    summed = tuple(
        (
            jnp.zeros((weight_piece.shape[0] * group_count,) + weight_piece.shape[1:], jnp.float32)
            for weight_piece in owned_shards
        )
    )
    outputs = []
    input_grads = []
    for micro_step in range(tokens.shape[0]):
        forward_set = (
            lax.all_gather(qkv_weight, "shard", axis=0, tiled=True),
            lax.all_gather(out_weight, "shard", axis=0, tiled=True),
            lax.all_gather(gate_weight, "shard", axis=0, tiled=True),
            lax.all_gather(up_weight, "shard", axis=0, tiled=True),
            lax.all_gather(down_weight, "shard", axis=0, tiled=True),
            lax.all_gather(norm1_gain, "shard", axis=0, tiled=True),
            lax.all_gather(norm1_bias, "shard", axis=0, tiled=True),
            lax.all_gather(norm2_gain, "shard", axis=0, tiled=True),
            lax.all_gather(norm2_bias, "shard", axis=0, tiled=True),
        )
        kept, layer_out = forward_pass(tokens[micro_step], segment_ids[micro_step], forward_set)
        backward_set = (
            lax.all_gather(qkv_weight, "shard", axis=0, tiled=True),
            lax.all_gather(out_weight, "shard", axis=0, tiled=True),
            lax.all_gather(gate_weight, "shard", axis=0, tiled=True),
            lax.all_gather(up_weight, "shard", axis=0, tiled=True),
            lax.all_gather(down_weight, "shard", axis=0, tiled=True),
            lax.all_gather(norm1_gain, "shard", axis=0, tiled=True),
            lax.all_gather(norm2_gain, "shard", axis=0, tiled=True),
        )
        grad_set, input_grad = backward_pass(
            kept, backward_set, out_grad[micro_step].astype(jnp.float32)
        )
        outputs.append(layer_out)
        input_grads.append(input_grad)
        summed = tuple((left_sum + right_sum for left_sum, right_sum in zip(summed, grad_set)))
    (
        sum_qkv,
        sum_out,
        sum_gate,
        sum_up,
        sum_down,
        sum_gain_one,
        sum_bias_one,
        sum_gain_two,
        sum_bias_two,
    ) = summed
    summed = (
        lax.psum_scatter(
            sum_qkv.astype(jnp.bfloat16), "shard", scatter_dimension=0, tiled=True
        ).astype(jnp.float32),
        lax.psum_scatter(
            sum_out.astype(jnp.bfloat16), "shard", scatter_dimension=0, tiled=True
        ).astype(jnp.float32),
        lax.psum_scatter(
            sum_gate.astype(jnp.bfloat16), "shard", scatter_dimension=0, tiled=True
        ).astype(jnp.float32),
        lax.psum_scatter(
            sum_up.astype(jnp.bfloat16), "shard", scatter_dimension=0, tiled=True
        ).astype(jnp.float32),
        lax.psum_scatter(
            sum_down.astype(jnp.bfloat16), "shard", scatter_dimension=0, tiled=True
        ).astype(jnp.float32),
        lax.psum_scatter(
            sum_gain_one.astype(jnp.bfloat16), "shard", scatter_dimension=0, tiled=True
        ).astype(jnp.float32),
        lax.psum_scatter(
            sum_bias_one.astype(jnp.bfloat16), "shard", scatter_dimension=0, tiled=True
        ).astype(jnp.float32),
        lax.psum_scatter(
            sum_gain_two.astype(jnp.bfloat16), "shard", scatter_dimension=0, tiled=True
        ).astype(jnp.float32),
        lax.psum_scatter(
            sum_bias_two.astype(jnp.bfloat16), "shard", scatter_dimension=0, tiled=True
        ).astype(jnp.float32),
    )
    (
        part_qkv,
        part_out,
        part_gate,
        part_up,
        part_down,
        part_gain_one,
        part_bias_one,
        part_gain_two,
        part_bias_two,
    ) = summed
    totals = (
        lax.psum(part_qkv.astype(jnp.bfloat16), "rep").astype(jnp.float32),
        lax.psum(part_out.astype(jnp.bfloat16), "rep").astype(jnp.float32),
        lax.psum(part_gate.astype(jnp.bfloat16), "rep").astype(jnp.float32),
        lax.psum(part_up.astype(jnp.bfloat16), "rep").astype(jnp.float32),
        lax.psum(part_down.astype(jnp.bfloat16), "rep").astype(jnp.float32),
        lax.psum(part_gain_one.astype(jnp.bfloat16), "rep").astype(jnp.float32),
        lax.psum(part_bias_one.astype(jnp.bfloat16), "rep").astype(jnp.float32),
        lax.psum(part_gain_two.astype(jnp.bfloat16), "rep").astype(jnp.float32),
        lax.psum(part_bias_two.astype(jnp.bfloat16), "rep").astype(jnp.float32),
    )
    return (
        jnp.stack(outputs),
        jnp.stack(input_grads),
        totals[0],
        totals[1],
        totals[2],
        totals[3],
        totals[4],
        totals[5],
        totals[6],
        totals[7],
        totals[8],
    )


def solution(mesh):
    in_specs = (
        P(None, ("shard", "rep"), None),
        P(None, ("shard", "rep")),
        P("shard", None),
        P("shard", None),
        P("shard", None),
        P("shard", None),
        P("shard", None),
        P("shard"),
        P("shard"),
        P("shard"),
        P("shard"),
        P(None, ("shard", "rep"), None),
    )
    out_specs = (
        P(None, ("shard", "rep"), None),
        P(None, ("shard", "rep"), None),
        P("shard", None),
        P("shard", None),
        P("shard", None),
        P("shard", None),
        P("shard", None),
        P("shard"),
        P("shard"),
        P("shard"),
        P("shard"),
    )
    return jax.shard_map(shards, mesh=mesh, in_specs=in_specs, out_specs=out_specs, check_vma=False)
```

profile of v0, /device:TPU:0, one launch (start us, length us, event | category | flops | bytes accessed | tf_op | source)
XLA Modules:
  0.0 871.6 jit_solution(1877780145343959413)
XLA Ops:
  14.7 15.5 %all-reduce.9 = (bf16[768]{0:T(1024)(128)(2,1)S(1)}, bf16[768]{0:T(1024)(128)(2,1)S(1)}, bf16[768]{0:T(1024)(128)(2,1)S(1)}) all-reduce(bf16[768]{0:T(1024)(128)(2,1)S(1)} %dynamic-update-slice.1, bf16[768]{0:T(1024)(128)(2,1)S(1)} %dynamic-update-slice, ...), channel_id=1, replica_groups=mesh['shard'=8,'rep'=4] {'shard'}, use_global_device_ids=true, to_apply=%add.1 | all-reduce | flops 2304 | bytes 9216
  30.6 16.1 %all-gather.6.cloned.1.call-done = bf16[768,2304]{1,0:T(8,128)(2,1)} async-done(((bf16[96,2304]{1,0:T(8,128)(2,1)}), bf16[768,2304]{1,0:T(8,128)(2,1)}) %all-gather.6.cloned.1.call-update) | async-done | bytes 3538960 | tf_op jit(solution)/shard_map/all_gather | solution.py:270
  46.8 4.3 fusion.135
  61.8 3.0 copy.65
  64.8 3.2 copy.66
  70.5 2.8 fusion.132
  78.6 33.0 %while.57 = (s32[]{:T(128)}, bf16[12,512,64]{1,2,0:T(8,128)(2,1)S(1)}, f32[12,512]{1,0:T(8,128)S(1)}, bf16[12,512,64]{2,1,0:T(8,128)(2,1)S(1)}, bf16[12,512,64]{...) while((s32[]{:T(128)}, ...), condition=%wide.region_11.12_spmd.clone, body=%wide.region_8.11_spmd.clone.sunk | while | flops 69467648 | bytes 3696737 | solution.py:120
  111.7 3.0 copy.68
  119.1 34.3 %while.56 = (s32[]{:T(128)}, bf16[12,512,64]{1,2,0:T(8,128)(2,1)S(1)}, f32[12,512]{1,0:T(8,128)S(1)}, bf16[12,512,64]{2,1,0:T(8,128)(2,1)}, bf16[12,512,64]{2,1,...) while((s32[]{:T(128)}, ...), condition=%wide.region_3.4_spmd.clone, body=%wide.region_0.3_spmd.clone.sunk | while | flops 69467648 | bytes 3696737 | solution.py:120
  153.5 2.7 fusion.176
  161.6 7.5 fusion.180
  169.1 9.0 %multiply_convert_fusion.6 = (bf16[512,3072]{1,0:T(8,128)(2,1)}, f32[512,3072]{1,0:T(8,128)}) fusion(f32[512,3072]{1,0:T(8,128)} %fusion.180, bf16[512,768]{1,0:T(8,128)(2,1)S(1)} %get-tuple-element.540, bf16[768,3072]{1,0:T(8,128)(2,1)} %all-gather.12.cloned.1.call-done), kind=kOutput, calls=%fused_computation.120 | convolution fusion | flops 2425356288 | bytes 21233664 | tf_op jit(solution)/shard_map/dot_general | solution.py:13
  178.1 16.9 %all-gather.14.cloned.1.call-done = bf16[3072,768]{1,0:T(8,128)(2,1)} async-done(((bf16[384,768]{1,0:T(8,128)(2,1)}), bf16[3072,768]{1,0:T(8,128)(2,1)}) %all-gather.14.cloned.1.call-update) | async-done | bytes 4718608 | tf_op jit(solution)/shard_map/all_gather | solution.py:274
  195.0 6.1 fusion.178
  202.3 2.6 fusion.179
  204.9 5.0 multiply_convert_fusion.7
  210.0 2.8 fusion.177
  217.0 9.5 %multiply_convert_fusion.4 = (bf16[512,3072]{1,0:T(8,128)(2,1)}, bf16[512,3072]{1,0:T(8,128)(2,1)}) fusion(f32[512,3072]{1,0:T(8,128)S(1)} %fusion.179, f32[512,3072]{1,0:T(8,128)} %get-tuple-element.553, bf16[3072,768]{1,0:T(8,128)(2,1)} %all-gather.14.cloned.1.call-done, f32[512]{0:T(512)S(1)} %broadcast_multiply_fusion.6, ...), kind=kOutput, calls=%fused_computation.118 | convolution fusion | flops 2439905280 | bytes 25964544 | tf_op jit(solution)/shard_map/dot_general | solution.py:23
  226.5 4.8 fusion.181
  231.3 7.1 multiply_reduce_fusion.3
  238.4 9.8 %multiply_convert_fusion.2 = (bf16[512,3072]{1,0:T(8,128)(2,1)}, bf16[512,3072]{1,0:T(8,128)(2,1)}) fusion(f32[512,3072]{1,0:T(8,128)S(1)} %bitcast.388, f32[512,3072]{1,0:T(8,128)} %get-tuple-element.557, bf16[3072,768]{1,0:T(8,128)(2,1)} %all-gather.14.cloned.1.call-done, f32[512]{0:T(512)S(1)} %broadcast_multiply_fusion.2, ...), kind=kOutput, calls=%fused_computation.116 | convolution fusion | flops 2439905280 | bytes 25964544 | tf_op jit(solution)/shard_map/dot_general | solution.py:23
  248.3 4.8 fusion.182
  253.1 7.2 multiply_reduce_fusion.2
  263.2 2.3 copy.77
  268.2 99.7 %while.58 = (s32[]{:T(128)}, f32[12,512,64]{1,2,0:T(8,128)}, f32[12,512,64]{1,2,0:T(8,128)}, bf16[12,512,64]{1,2,0:T(8,128)(2,1)}, bf16[12,512,64]{2,1,0:T(8,128...) while((s32[]{:T(128)}, f32[12,512,64]{1,2,0:T(8,128)}, ...), condition=%wide.region_22.23_spmd.clone, body=%wide.region_20.22_spmd.clone.sunk | while | flops 170458624 | bytes 9063537 | solution.py:202
  374.6 92.3 %while.59 = (s32[]{:T(128)}, f32[12,512,64]{1,2,0:T(8,128)S(1)}, f32[12,512,64]{1,2,0:T(8,128)}, bf16[12,512,64]{1,2,0:T(8,128)(2,1)}, bf16[12,512,64]{2,1,0:T(8...) while((s32[]{:T(128)}, f32[12,512,64]{1,2,0:T(8,128)S(1)}, ...), condition=%wide.region_29.30_spmd.clone, body=%wide.region_27.29_spmd.clone.sunk | while | flops 170458624 | bytes 9063537 | solution.py:202
  466.9 3.1 multiply_bitcast_fusion.3
  472.9 2.9 fusion.119
  475.7 4.5 fusion.127
  480.3 5.1 fusion.92
  485.4 5.8 copy.88
  492.3 2.3 fusion.149
  496.8 6.0 fusion.152
  502.8 5.4 add_convert_fusion
  509.4 4.7 fusion.184
  514.1 4.6 add_convert_fusion.1
  519.1 4.7 fusion.183
  523.8 4.6 add_convert_fusion.2
  530.2 9.3 %reduce-scatter.16.cloned.1.call-done = bf16[96,2304]{1,0:T(8,128)(2,1)} async-done(((bf16[768,2304]{1,0:T(8,128)(2,1)}), bf16[96,2304]{1,0:T(8,128)(2,1)}) %reduce-scatter.16.cloned.1.call-update) | async-done | bytes 442384
  541.5 38.5 %reduce-scatter.8.cloned.1.call-done = bf16[96,768]{1,0:T(8,128)(2,1)} async-done(((bf16[768,768]{1,0:T(8,128)(2,1)}), bf16[96,768]{1,0:T(8,128)(2,1)}) %reduce-scatter.8.cloned.1.call-update) | async-done | bytes 147472 | tf_op jit(solution)/shard_map/reduce_scatter | solution.py:311
  580.0 57.8 %reduce-scatter.14.cloned.1.call-done = bf16[384,768]{1,0:T(8,128)(2,1)} async-done(((bf16[3072,768]{1,0:T(8,128)(2,1)}), bf16[384,768]{1,0:T(8,128)(2,1)}) %reduce-scatter.14.cloned.1.call-update) | async-done | bytes 589840 | tf_op jit(solution)/shard_map/reduce_scatter | solution.py:320
  637.8 57.4 %reduce-scatter.12.cloned.1.call-done = bf16[96,3072]{1,0:T(8,128)(2,1)} async-done(((bf16[768,3072]{1,0:T(8,128)(2,1)}), bf16[96,3072]{1,0:T(8,128)(2,1)}) %reduce-scatter.12.cloned.1.call-update) | async-done | bytes 589840 | tf_op jit(solution)/shard_map/reduce_scatter | solution.py:317
  695.2 57.6 %reduce-scatter.10.cloned.1.call-done = bf16[96,3072]{1,0:T(8,128)(2,1)} async-done(((bf16[768,3072]{1,0:T(8,128)(2,1)}), bf16[96,3072]{1,0:T(8,128)(2,1)}) %reduce-scatter.10.cloned.1.call-update) | async-done | bytes 589840 | tf_op jit(solution)/shard_map/reduce_scatter | solution.py:314
  752.9 23.9 %all-reduce.8 = (bf16[768]{0:T(1024)(128)(2,1)S(1)}, bf16[768]{0:T(1024)(128)(2,1)S(1)}, bf16[768]{0:T(1024)(128)(2,1)S(1)}, bf16[768]{0:T(1024)(128)(2,1)S(1)}, bf16[768]{0:T(1024)(128)(2,1)S(1)}) all-reduce(bf16[768]{0:T(1024)(128)(2,1)S(1)} %dynamic-update-slice.3, ...), channel_id=1, replica_groups=mesh['shard'=8,'rep'=4] {'shard'}, use_global_device_ids=true, to_apply=%add.3 | all-reduce | flops 3840 | bytes 15360
  777.1 12.4 %all-reduce.10 = (bf16[96]{0:T(256)(128)(2,1)S(1)}, bf16[96]{0:T(256)(128)(2,1)S(1)}, bf16[96]{0:T(256)(128)(2,1)S(1)}, bf16[96]{0:T(256)(128)(2,1)S(1)}) all-reduce(bf16[96]{0:T(256)(128)(2,1)S(1)} %dynamic-slice.5, bf16[96]{0:T(256)(128)(2,1)S(1)} %dynamic-slice.7, ...), channel_id=1, replica_groups=mesh['shard'=8,'rep'=4] {'rep'}, use_global_device_ids=true, to_apply=%region_43.44 | all-reduce | flops 384 | bytes 1536 | tf_op jit(solution)/shard_map/psum | solution.py:353
  791.5 4.9 fusion.125
  796.5 3.2 fusion.126
  803.5 54.9 %all-reduce.14.cloned.1.call-done = (bf16[96,2304]{0,1:T(8,128)(2,1)}, bf16[96,768]{1,0:T(8,128)(2,1)}, bf16[96,3072]{1,0:T(8,128)(2,1)}, bf16[96,3072]{1,0:T(8,128)(2,1)}, bf16[384,768]{1,0:T(8,128)(2,1)}) async-done(((bf16[96,2304]{0,1:T(8,128)(2,1)}, bf16[96,768]{1,0:T(8,128)(2,1)}, bf16[96,3072]{1,0:T(8,128)(2,1)}, bf16[96,3072]{1,0:T(8,128)(2,1)}, bf16[384,768]{1,0:T(8,128)(2,1)}), ...) | async-done | bytes 2359312 | tf_op jit(solution)/shard_map/psum | solution.py:348
  (574 shorter events, 333.0 us)
Async XLA Ops:
  7.2 39.6 %all-gather.6.cloned.1.call-start = ((), (), s32[]{:S(2)}) async-start(), calls=%async_computation.5 | async-start | bytes 3981312 | tf_op jit(solution)/shard_map/all_gather | solution.py:270
  7.9 145.5 %all-gather.8.cloned.1.call-start = ((), (), s32[]{:S(2)}) async-start(), calls=%async_computation.6 | async-start | bytes 1327104 | tf_op jit(solution)/shard_map/all_gather | solution.py:271
  8.7 152.9 %all-gather.10.cloned.1.call-start = ((), (), s32[]{:S(2)}) async-start(), calls=%async_computation.7 | async-start | bytes 5308416 | tf_op jit(solution)/shard_map/all_gather | solution.py:272
  9.4 159.7 %all-gather.12.cloned.1.call-start = ((), (), s32[]{:S(2)}) async-start(), calls=%async_computation.8 | async-start | bytes 5308416 | tf_op jit(solution)/shard_map/all_gather | solution.py:273
  10.0 185.0 %all-gather.14.cloned.1.call-start = ((), (), s32[]{:S(2)}) async-start(), calls=%async_computation.9 | async-start | bytes 5308416 | tf_op jit(solution)/shard_map/all_gather | solution.py:274
  10.6 528.9 %reduce-scatter.16.cloned.1.call-start = ((), (), s32[]{:S(2)}) async-start(), calls=%async_computation.14 | async-start | bytes 3981312
  30.6 39.9 %copy-start.38 = (f32[512,64]{0,1:T(8,128)}, f32[512,64]{0,1:T(8,128)S(1)}, u32[]{:S(2)}) copy-start(f32[512,64]{0,1:T(8,128)S(1)} %get-tuple-element.562) | copy-start | bytes 393220
  30.6 39.9 %copy-start.40 = (f32[512,64]{0,1:T(8,128)}, f32[512,64]{0,1:T(8,128)S(1)}, u32[]{:S(2)}) copy-start(f32[512,64]{0,1:T(8,128)S(1)} %get-tuple-element.563) | copy-start | bytes 393220
  111.6 4.5 copy-start.4
  111.6 4.5 copy-start.29
  119.1 34.3 %copy-start.5 = (bf16[12,512,64]{1,2,0:T(8,128)(2,1)S(1)}, bf16[12,512,64]{1,2,0:T(8,128)(2,1)}, u32[]{:S(2)}) copy-start(bf16[12,512,64]{1,2,0:T(8,128)(2,1)} %copy-done.4) | copy-start | bytes 2359300
  161.6 7.5 copy-start.32
  169.1 25.9 %copy-start.11 = (f32[512,768]{1,0:T(8,128)S(1)}, f32[512,768]{1,0:T(8,128)}, u32[]{:S(2)}) copy-start(f32[512,768]{1,0:T(8,128)} %copy-done.10) | copy-start | bytes 4718596
  195.0 6.5 slice-start
  195.0 6.5 slice-start.1
  202.3 7.7 slice-start.6
  204.9 5.1 copy-start.23
  204.9 5.1 slice-start.7
  212.8 18.5 %copy-start.8 = (f32[512,768]{1,0:T(8,128)}, f32[512,768]{1,0:T(8,128)S(1)}, u32[]{:S(2)}) copy-start(f32[512,768]{1,0:T(8,128)S(1)} %get-tuple-element.555) | copy-start | bytes 4718596
  226.5 4.8 copy-start.24
  226.5 4.8 copy-start.35
  226.5 11.9 %slice-start.2 = ((s8[6291456]{0:T(1024)(128)(4,1)}), s8[4194304]{0:T(1024)(128)(4,1)S(1)}, s32[]{:S(2)}) async-start(s8[6291456]{0:T(1024)(128)(4,1)} %bitcast.387), calls=%async_computation.18 | async-start | bytes 8388608
  231.3 7.1 slice-start.3
  248.2 4.8 copy-start.25
  248.2 4.8 copy-start.68
  248.2 4.8 copy-start.71
  253.1 8.5 copy-start.60
  374.6 92.3 %copy-start.41 = (f32[512,64]{0,1:T(8,128)S(1)}, f32[512,64]{0,1:T(8,128)}, u32[]{:S(2)}) copy-start(f32[512,64]{0,1:T(8,128)} %copy-done.40) | copy-start | bytes 393220
  475.7 4.5 copy-start.42
  475.7 4.5 copy-start.44
  475.7 4.6 copy-start.58
  491.3 88.8 %reduce-scatter.8.cloned.1.call-start = ((), (), s32[]{:S(2)}) async-start(), calls=%async_computation.10 | async-start | bytes 1327104 | tf_op jit(solution)/shard_map/reduce_scatter | solution.py:311
  496.5 6.3 copy-start.20
  496.5 141.3 %reduce-scatter.14.cloned.1.call-start = ((), (), s32[]{:S(2)}) async-start(), calls=%async_computation.13 | async-start | bytes 5308416 | tf_op jit(solution)/shard_map/reduce_scatter | solution.py:320
  496.8 6.1 copy-start.70
  508.2 5.9 copy-start.33
  508.3 186.9 %reduce-scatter.12.cloned.1.call-start = ((), (), s32[]{:S(2)}) async-start(), calls=%async_computation.12 | async-start | bytes 5308416 | tf_op jit(solution)/shard_map/reduce_scatter | solution.py:317
  509.4 4.8 copy-start.69
  518.8 234.0 %reduce-scatter.10.cloned.1.call-start = ((), (), s32[]{:S(2)}) async-start(), calls=%async_computation.11 | async-start | bytes 5308416 | tf_op jit(solution)/shard_map/reduce_scatter | solution.py:314
  519.0 4.8 copy-start.67
  528.4 330.1 %all-reduce.14.cloned.1.call-start = ((), (), s32[]{:S(2)}) async-start(), calls=%async_computation.15 | async-start | bytes 5013504 | tf_op jit(solution)/shard_map/psum | solution.py:348
  530.1 222.7 %copy-start.50 = (f32[768]{0:T(1024)S(1)}, f32[768]{0:T(1024)}, u32[]{:S(2)}) copy-start(f32[768]{0:T(1024)} %get-tuple-element.388) | copy-start | bytes 9220
  530.1 222.7 %copy-start.51 = (f32[768]{0:T(1024)S(1)}, f32[768]{0:T(1024)}, u32[]{:S(2)}) copy-start(f32[768]{0:T(1024)} %get-tuple-element.397) | copy-start | bytes 9220
  530.1 261.4 %copy-start.37 = (f32[512,768]{1,0:T(8,128)S(1)}, f32[512,768]{1,0:T(8,128)}, u32[]{:S(2)}) copy-start(f32[512,768]{1,0:T(8,128)} %copy-done.36) | copy-start | bytes 4718596
  791.5 4.9 copy-start.28
  791.5 4.9 copy-start.43
  791.5 5.0 copy-start.45
  791.5 5.0 copy-start.55
  (43 other events, 92.1 us)
Sparse Core Ops, SparseCore 0:
  9.9 36.8 all-gather.5
  48.7 24.0 all-gather.7
  74.6 38.9 all-gather.9
  115.3 38.9 all-gather.11
  156.0 38.9 all-gather.13
  491.4 48.0 reduce-scatter.15
  543.3 36.7 reduce-scatter.7
  583.9 53.8 reduce-scatter.13
  641.3 53.8 reduce-scatter.11
  698.9 53.9 reduce-scatter.9
  756.2 102.2 all-reduce.13
where the time goes:
time: 885 us; the launch traced here: 872 us
  matrix products  385 us (44%)
  waiting for transfers between devices  312 us (35%)
  local copies, waits for them, and re-layouts  64 us (7%)
  blocking collectives  51.8 us (6%)
  other arithmetic  39.6 us (4%)
  between operations  16.6 us (2%)
    dot_general x82, matrix products, times_transposed(): lax.dot_general(left_op, right_op, (((1,), (1,)), ((), ())), preferred_el...  147 us
    dot_general x58, matrix products, inner_sum(): lax.dot_general(left_op, right_op, (((0,), (0,)), ((), ())), preferred_el...  130 us
    dot_general x58, matrix products, matmul(): return jnp.dot(left_op, right_op, preferred_element_type=jnp.float32)  108 us
    reduce_scatter x1, waiting for transfers between devices, shards(): lax.psum_scatter(sum_down.astype(jnp.bfloat16), 'shard', scatter_dimensio...  57.8 us
    reduce_scatter x1, waiting for transfers between devices, shards(): lax.psum_scatter(sum_gate.astype(jnp.bfloat16), 'shard', scatter_dimensio...  57.6 us
    reduce_scatter x1, waiting for transfers between devices, shards(): lax.psum_scatter(sum_up.astype(jnp.bfloat16), 'shard', scatter_dimension=...  57.4 us
    psum x1, waiting for transfers between devices, shards(): lax.psum(part_qkv.astype(jnp.bfloat16), 'rep').astype(jnp.float32)  54.9 us
    unnamed x2, blocking collectives  39.4 us
  transfers between devices with their start and end apart: 11, of which 8 were waited for; matrix products, arithmetic and copies ran while one was open for 20% of the time, Pallas kernels for 0%

commit v1 on v0

--- a/solution.py
+++ b/solution.py
@@ -345,7 +345,7 @@
         part_bias_two,
     ) = summed
     totals = (
-        lax.psum(part_qkv.astype(jnp.bfloat16), "rep").astype(jnp.float32),
+        jnp.sum(lax.all_gather(part_qkv.astype(jnp.bfloat16), "rep"), axis=0).astype(jnp.float32),
         lax.psum(part_out.astype(jnp.bfloat16), "rep").astype(jnp.float32),
         lax.psum(part_gate.astype(jnp.bfloat16), "rep").astype(jnp.float32),
         lax.psum(part_up.astype(jnp.bfloat16), "rep").astype(jnp.float32),

time: 885 us -> 903 us (1.020)
  waiting for transfers between devices: 312 us -> 332 us
    psum x1, waiting for transfers between devices: 54.9 us -> 72.3 us  [shards(): lax.psum(part_out.astype(jnp.bfloat16), 'rep').astype(jnp.float32)]
    reduce_scatter x0 -> x1, waiting for transfers between devices: none -> 11.1 us  [shards(): lax.psum_scatter(sum_qkv.astype(jnp.bfloat16), 'shard', scatter_dimension...]
    unnamed x12, waiting for transfers between devices: 12.5 us -> 3.23 us
    unnamed x184 -> x180, local copies, waits for them, and re-layouts: 39.2 us -> 35.4 us
  transfers between devices with their start and end apart: 11 -> 12, of which waited for: 8 -> 8; matrix products, arithmetic and copies ran while one was open for 20% -> 20% of each run, Pallas kernels for 0% -> 0%
where the time goes in v1:
time: 903 us; the launch traced here: 890 us
  matrix products  384 us (43%)
  waiting for transfers between devices  332 us (37%)
  local copies, waits for them, and re-layouts  60.3 us (7%)
  blocking collectives  51.4 us (6%)
  other arithmetic  42.4 us (5%)
  between operations  16.9 us (2%)
    dot_general x82, matrix products, times_transposed(): lax.dot_general(left_op, right_op, (((1,), (1,)), ((), ())), preferred_el...  147 us
    dot_general x58, matrix products, inner_sum(): lax.dot_general(left_op, right_op, (((0,), (0,)), ((), ())), preferred_el...  130 us
    dot_general x58, matrix products, matmul(): return jnp.dot(left_op, right_op, preferred_element_type=jnp.float32)  108 us
    psum x1, waiting for transfers between devices, shards(): lax.psum(part_out.astype(jnp.bfloat16), 'rep').astype(jnp.float32)  72.3 us
    reduce_scatter x1, waiting for transfers between devices, shards(): lax.psum_scatter(sum_down.astype(jnp.bfloat16), 'shard', scatter_dimensio...  57.8 us
    reduce_scatter x1, waiting for transfers between devices, shards(): lax.psum_scatter(sum_gate.astype(jnp.bfloat16), 'shard', scatter_dimensio...  57.6 us
    reduce_scatter x1, waiting for transfers between devices, shards(): lax.psum_scatter(sum_up.astype(jnp.bfloat16), 'shard', scatter_dimension=...  57.4 us
    unnamed x2, blocking collectives  39.4 us
  transfers between devices with their start and end apart: 12, of which 8 were waited for; matrix products, arithmetic and copies ran while one was open for 20% of the time, Pallas kernels for 0%

profile of v1, /device:TPU:0, one launch (start us, length us, event | category | flops | bytes accessed | tf_op | source)
XLA Modules:
  0.0 890.1 jit_solution(7933489836990425746)
XLA Ops:
  14.7 15.5 %all-reduce.9 = (bf16[768]{0:T(1024)(128)(2,1)S(1)}, bf16[768]{0:T(1024)(128)(2,1)S(1)}, bf16[768]{0:T(1024)(128)(2,1)S(1)}) all-reduce(bf16[768]{0:T(1024)(128)(2,1)S(1)} %dynamic-update-slice.1, bf16[768]{0:T(1024)(128)(2,1)S(1)} %dynamic-update-slice, ...), channel_id=1, replica_groups=mesh['shard'=8,'rep'=4] {'shard'}, use_global_device_ids=true, to_apply=%add.1 | all-reduce | flops 2304 | bytes 9216
  30.6 16.1 %all-gather.8.cloned.1.call-done = bf16[768,2304]{1,0:T(8,128)(2,1)} async-done(((bf16[96,2304]{1,0:T(8,128)(2,1)}), bf16[768,2304]{1,0:T(8,128)(2,1)}) %all-gather.8.cloned.1.call-update) | async-done | bytes 3538960 | tf_op jit(solution)/shard_map/all_gather | solution.py:270
  46.8 4.3 fusion.135
  61.8 3.0 copy.64
  64.8 3.2 copy.65
  70.5 2.8 fusion.132
  78.6 33.1 %while.57 = (s32[]{:T(128)}, bf16[12,512,64]{1,2,0:T(8,128)(2,1)S(1)}, f32[12,512]{1,0:T(8,128)S(1)}, bf16[12,512,64]{2,1,0:T(8,128)(2,1)S(1)}, bf16[12,512,64]{...) while((s32[]{:T(128)}, ...), condition=%wide.region_11.12_spmd.clone, body=%wide.region_8.11_spmd.clone.sunk | while | flops 69467648 | bytes 3696737 | solution.py:120
  111.7 3.0 copy.67
  119.2 34.3 %while.56 = (s32[]{:T(128)}, bf16[12,512,64]{1,2,0:T(8,128)(2,1)S(1)}, f32[12,512]{1,0:T(8,128)S(1)}, bf16[12,512,64]{2,1,0:T(8,128)(2,1)}, bf16[12,512,64]{2,1,...) while((s32[]{:T(128)}, ...), condition=%wide.region_3.4_spmd.clone, body=%wide.region_0.3_spmd.clone.sunk | while | flops 69467648 | bytes 3696737 | solution.py:120
  153.5 2.7 fusion.176
  161.7 7.4 fusion.180
  169.1 9.0 %multiply_convert_fusion.6 = (bf16[512,3072]{1,0:T(8,128)(2,1)}, f32[512,3072]{1,0:T(8,128)}) fusion(f32[512,3072]{1,0:T(8,128)} %fusion.180, bf16[512,768]{1,0:T(8,128)(2,1)S(1)} %get-tuple-element.506, bf16[768,3072]{1,0:T(8,128)(2,1)} %all-gather.14.cloned.1.call-done), kind=kOutput, calls=%fused_computation.120 | convolution fusion | flops 2425356288 | bytes 21233664 | tf_op jit(solution)/shard_map/dot_general | solution.py:13
  178.1 16.9 %all-gather.16.cloned.1.call-done = bf16[3072,768]{1,0:T(8,128)(2,1)} async-done(((bf16[384,768]{1,0:T(8,128)(2,1)}), bf16[3072,768]{1,0:T(8,128)(2,1)}) %all-gather.16.cloned.1.call-update) | async-done | bytes 4718608 | tf_op jit(solution)/shard_map/all_gather | solution.py:274
  195.0 6.1 fusion.178
  202.3 2.6 fusion.179
  204.9 5.0 multiply_convert_fusion.7
  210.0 2.8 fusion.177
  217.0 9.5 %multiply_convert_fusion.4 = (bf16[512,3072]{1,0:T(8,128)(2,1)}, bf16[512,3072]{1,0:T(8,128)(2,1)}) fusion(f32[512,3072]{1,0:T(8,128)S(1)} %fusion.179, f32[512,3072]{1,0:T(8,128)} %get-tuple-element.519, bf16[3072,768]{1,0:T(8,128)(2,1)} %all-gather.16.cloned.1.call-done, f32[512]{0:T(512)S(1)} %broadcast_multiply_fusion.6, ...), kind=kOutput, calls=%fused_computation.118 | convolution fusion | flops 2439905280 | bytes 25964544 | tf_op jit(solution)/shard_map/dot_general | solution.py:23
  226.5 4.8 fusion.181
  231.3 7.1 multiply_reduce_fusion.3
  238.4 9.8 %multiply_convert_fusion.2 = (bf16[512,3072]{1,0:T(8,128)(2,1)}, bf16[512,3072]{1,0:T(8,128)(2,1)}) fusion(f32[512,3072]{1,0:T(8,128)S(1)} %bitcast.389, f32[512,3072]{1,0:T(8,128)} %get-tuple-element.523, bf16[3072,768]{1,0:T(8,128)(2,1)} %all-gather.16.cloned.1.call-done, f32[512]{0:T(512)S(1)} %broadcast_multiply_fusion.2, ...), kind=kOutput, calls=%fused_computation.116 | convolution fusion | flops 2439905280 | bytes 25964544 | tf_op jit(solution)/shard_map/dot_general | solution.py:23
  248.2 4.8 fusion.182
  253.1 7.2 multiply_reduce_fusion.2
  263.2 2.3 copy.76
  268.2 99.5 %while.58 = (s32[]{:T(128)}, f32[12,512,64]{1,2,0:T(8,128)}, f32[12,512,64]{1,2,0:T(8,128)}, bf16[12,512,64]{1,2,0:T(8,128)(2,1)}, bf16[12,512,64]{2,1,0:T(8,128...) while((s32[]{:T(128)}, f32[12,512,64]{1,2,0:T(8,128)}, ...), condition=%wide.region_22.23_spmd.clone, body=%wide.region_20.22_spmd.clone.sunk | while | flops 170458624 | bytes 9063537 | solution.py:202
  374.3 92.2 %while.59 = (s32[]{:T(128)}, f32[12,512,64]{1,2,0:T(8,128)S(1)}, f32[12,512,64]{1,2,0:T(8,128)}, bf16[12,512,64]{1,2,0:T(8,128)(2,1)}, bf16[12,512,64]{2,1,0:T(8...) while((s32[]{:T(128)}, f32[12,512,64]{1,2,0:T(8,128)S(1)}, ...), condition=%wide.region_29.30_spmd.clone, body=%wide.region_27.29_spmd.clone.sunk | while | flops 170458624 | bytes 9063537 | solution.py:202
  466.5 3.1 multiply_bitcast_fusion.3
  472.5 2.9 fusion.119
  475.4 4.5 fusion.127
  480.0 5.1 fusion.92
  485.1 5.8 copy.87
  492.0 2.3 fusion.149
  496.4 6.0 fusion.152
  502.5 5.4 add_convert_fusion
  509.0 4.7 fusion.184
  513.8 4.6 add_convert_fusion.1
  518.6 4.7 fusion.183
  523.4 4.6 add_convert_fusion.2
  528.1 11.1 %reduce-scatter.16.cloned.1.call-done = bf16[96,2304]{1,0:T(8,128)(2,1)} async-done(((bf16[768,2304]{1,0:T(8,128)(2,1)}), bf16[96,2304]{1,0:T(8,128)(2,1)}) %reduce-scatter.16.cloned.1.call-update) | async-done | bytes 442384 | tf_op jit(solution)/shard_map/reduce_scatter | solution.py:308
  540.5 39.3 %reduce-scatter.8.cloned.1.call-done = bf16[96,768]{1,0:T(8,128)(2,1)} async-done(((bf16[768,768]{1,0:T(8,128)(2,1)}), bf16[96,768]{1,0:T(8,128)(2,1)}) %reduce-scatter.8.cloned.1.call-update) | async-done | bytes 147472 | tf_op jit(solution)/shard_map/reduce_scatter | solution.py:311
  579.7 57.8 %reduce-scatter.14.cloned.1.call-done = bf16[384,768]{1,0:T(8,128)(2,1)} async-done(((bf16[3072,768]{1,0:T(8,128)(2,1)}), bf16[384,768]{1,0:T(8,128)(2,1)}) %reduce-scatter.14.cloned.1.call-update) | async-done | bytes 589840 | tf_op jit(solution)/shard_map/reduce_scatter | solution.py:320
  637.5 57.4 %reduce-scatter.12.cloned.1.call-done = bf16[96,3072]{1,0:T(8,128)(2,1)} async-done(((bf16[768,3072]{1,0:T(8,128)(2,1)}), bf16[96,3072]{1,0:T(8,128)(2,1)}) %reduce-scatter.12.cloned.1.call-update) | async-done | bytes 589840 | tf_op jit(solution)/shard_map/reduce_scatter | solution.py:317
  694.9 57.6 %reduce-scatter.10.cloned.1.call-done = bf16[96,3072]{1,0:T(8,128)(2,1)} async-done(((bf16[768,3072]{1,0:T(8,128)(2,1)}), bf16[96,3072]{1,0:T(8,128)(2,1)}) %reduce-scatter.10.cloned.1.call-update) | async-done | bytes 589840 | tf_op jit(solution)/shard_map/reduce_scatter | solution.py:314
  752.5 23.9 %all-reduce.8 = (bf16[768]{0:T(1024)(128)(2,1)S(1)}, bf16[768]{0:T(1024)(128)(2,1)S(1)}, bf16[768]{0:T(1024)(128)(2,1)S(1)}, bf16[768]{0:T(1024)(128)(2,1)S(1)}, bf16[768]{0:T(1024)(128)(2,1)S(1)}) all-reduce(bf16[768]{0:T(1024)(128)(2,1)S(1)} %dynamic-update-slice.3, ...), channel_id=1, replica_groups=mesh['shard'=8,'rep'=4] {'shard'}, use_global_device_ids=true, to_apply=%add.3 | all-reduce | flops 3840 | bytes 15360
  776.7 12.0 %all-reduce.10 = (bf16[96]{0:T(256)(128)(2,1)S(1)}, bf16[96]{0:T(256)(128)(2,1)S(1)}, bf16[96]{0:T(256)(128)(2,1)S(1)}, bf16[96]{0:T(256)(128)(2,1)S(1)}) all-reduce(bf16[96]{0:T(256)(128)(2,1)S(1)} %dynamic-slice.5, bf16[96]{0:T(256)(128)(2,1)S(1)} %dynamic-slice.7, ...), channel_id=1, replica_groups=mesh['shard'=8,'rep'=4] {'rep'}, use_global_device_ids=true, to_apply=%region_43.44 | all-reduce | flops 384 | bytes 1536 | tf_op jit(solution)/shard_map/psum | solution.py:353
  790.8 4.9 fusion.125
  795.8 3.2 fusion.126
  805.5 72.3 %all-reduce.14.cloned.1.call-done = (bf16[96,768]{1,0:T(8,128)(2,1)}, bf16[96,3072]{1,0:T(8,128)(2,1)}, bf16[96,3072]{1,0:T(8,128)(2,1)}, bf16[384,768]{1,0:T(8,128)(2,1)}) async-done(((bf16[96,768]{1,0:T(8,128)(2,1)}, bf16[96,3072]{1,0:T(8,128)(2,1)}, bf16[96,3072]{1,0:T(8,128)(2,1)}, bf16[384,768]{1,0:T(8,128)(2,1)}), (bf16[96,768]{1,0:T(8,128)(2,1)}, bf16[96,3072]{1,0:T(8,128)(2,1)}, ...) | async-done | bytes 1916944 | tf_op jit(solution)/shard_map/psum | solution.py:349
  (575 shorter events, 331.8 us)
Async XLA Ops:
  7.2 39.6 %all-gather.8.cloned.1.call-start = ((), (), s32[]{:S(2)}) async-start(), calls=%async_computation.5 | async-start | bytes 3981312 | tf_op jit(solution)/shard_map/all_gather | solution.py:270
  7.9 145.6 %all-gather.10.cloned.1.call-start = ((), (), s32[]{:S(2)}) async-start(), calls=%async_computation.6 | async-start | bytes 1327104 | tf_op jit(solution)/shard_map/all_gather | solution.py:271
  8.7 153.0 %all-gather.12.cloned.1.call-start = ((), (), s32[]{:S(2)}) async-start(), calls=%async_computation.7 | async-start | bytes 5308416 | tf_op jit(solution)/shard_map/all_gather | solution.py:272
  9.4 159.7 %all-gather.14.cloned.1.call-start = ((), (), s32[]{:S(2)}) async-start(), calls=%async_computation.8 | async-start | bytes 5308416 | tf_op jit(solution)/shard_map/all_gather | solution.py:273
  10.0 185.0 %all-gather.16.cloned.1.call-start = ((), (), s32[]{:S(2)}) async-start(), calls=%async_computation.9 | async-start | bytes 5308416 | tf_op jit(solution)/shard_map/all_gather | solution.py:274
  10.6 528.6 %reduce-scatter.16.cloned.1.call-start = ((), (), s32[]{:S(2)}) async-start(), calls=%async_computation.15 | async-start | bytes 3981312 | tf_op jit(solution)/shard_map/reduce_scatter | solution.py:308
  30.6 39.9 %copy-start.38 = (f32[512,64]{0,1:T(8,128)}, f32[512,64]{0,1:T(8,128)S(1)}, u32[]{:S(2)}) copy-start(f32[512,64]{0,1:T(8,128)S(1)} %get-tuple-element.528) | copy-start | bytes 393220
  30.6 39.9 %copy-start.40 = (f32[512,64]{0,1:T(8,128)}, f32[512,64]{0,1:T(8,128)S(1)}, u32[]{:S(2)}) copy-start(f32[512,64]{0,1:T(8,128)S(1)} %get-tuple-element.529) | copy-start | bytes 393220
  119.2 34.3 %copy-start.5 = (bf16[12,512,64]{1,2,0:T(8,128)(2,1)S(1)}, bf16[12,512,64]{1,2,0:T(8,128)(2,1)}, u32[]{:S(2)}) copy-start(bf16[12,512,64]{1,2,0:T(8,128)(2,1)} %copy-done.4) | copy-start | bytes 2359300
  161.7 7.4 copy-start.32
  169.1 25.9 %copy-start.11 = (f32[512,768]{1,0:T(8,128)S(1)}, f32[512,768]{1,0:T(8,128)}, u32[]{:S(2)}) copy-start(f32[512,768]{1,0:T(8,128)} %copy-done.10) | copy-start | bytes 4718596
  195.0 6.5 slice-start
  195.0 6.5 slice-start.1
  202.3 7.7 slice-start.6
  204.9 5.0 copy-start.23
  204.9 5.0 slice-start.7
  212.8 18.5 %copy-start.8 = (f32[512,768]{1,0:T(8,128)}, f32[512,768]{1,0:T(8,128)S(1)}, u32[]{:S(2)}) copy-start(f32[512,768]{1,0:T(8,128)S(1)} %get-tuple-element.521) | copy-start | bytes 4718596
  226.5 4.8 copy-start.24
  226.5 4.8 copy-start.35
  226.5 11.9 %slice-start.2 = ((s8[6291456]{0:T(1024)(128)(4,1)}), s8[4194304]{0:T(1024)(128)(4,1)S(1)}, s32[]{:S(2)}) async-start(s8[6291456]{0:T(1024)(128)(4,1)} %bitcast.388), calls=%async_computation.19 | async-start | bytes 8388608
  231.3 7.1 slice-start.3
  248.2 4.8 copy-start.25
  248.2 4.8 copy-start.67
  248.2 4.8 copy-start.70
  253.1 8.5 copy-start.59
  374.3 92.2 %copy-start.41 = (f32[512,64]{0,1:T(8,128)S(1)}, f32[512,64]{0,1:T(8,128)}, u32[]{:S(2)}) copy-start(f32[512,64]{0,1:T(8,128)} %copy-done.40) | copy-start | bytes 393220
  475.4 4.5 copy-start.44
  475.4 4.6 copy-start.57
  490.9 88.8 %reduce-scatter.8.cloned.1.call-start = ((), (), s32[]{:S(2)}) async-start(), calls=%async_computation.10 | async-start | bytes 1327104 | tf_op jit(solution)/shard_map/reduce_scatter | solution.py:311
  496.2 6.3 copy-start.20
  496.2 141.3 %reduce-scatter.14.cloned.1.call-start = ((), (), s32[]{:S(2)}) async-start(), calls=%async_computation.13 | async-start | bytes 5308416 | tf_op jit(solution)/shard_map/reduce_scatter | solution.py:320
  496.4 6.1 copy-start.69
  507.9 5.9 copy-start.33
  507.9 187.0 %reduce-scatter.12.cloned.1.call-start = ((), (), s32[]{:S(2)}) async-start(), calls=%async_computation.12 | async-start | bytes 5308416 | tf_op jit(solution)/shard_map/reduce_scatter | solution.py:317
  509.0 4.8 copy-start.68
  518.4 234.1 %reduce-scatter.10.cloned.1.call-start = ((), (), s32[]{:S(2)}) async-start(), calls=%async_computation.11 | async-start | bytes 5308416 | tf_op jit(solution)/shard_map/reduce_scatter | solution.py:314
  518.6 4.8 copy-start.66
  528.0 11.3 %copy-start.64 = (bf16[96]{0:T(256)(128)(2,1)S(1)}, bf16[96]{0:T(256)(128)(2,1)}, u32[]{:S(2)}) copy-start(bf16[96]{0:T(256)(128)(2,1)} %param.30) | copy-start | bytes 580
  528.0 12.2 %copy-start.21 = (bf16[2,512,768]{2,1,0:T(8,128)(2,1)S(1)}, bf16[2,512,768]{2,1,0:T(8,128)(2,1)}, u32[]{:S(2)}) copy-start(bf16[2,512,768]{2,1,0:T(8,128)(2,1)} %param.31) | copy-start | bytes 4718596
  528.0 12.4 %copy-start.49 = (f32[768]{0:T(1024)S(1)}, f32[768]{0:T(1024)}, u32[]{:S(2)}) copy-start(f32[768]{0:T(1024)} %get-tuple-element.355) | copy-start | bytes 9220
  528.0 12.4 %copy-start.50 = (f32[768]{0:T(1024)S(1)}, f32[768]{0:T(1024)}, u32[]{:S(2)}) copy-start(f32[768]{0:T(1024)} %get-tuple-element.364) | copy-start | bytes 9220
  528.0 274.8 %all-gather.18.cloned.1.call-start = ((), (), s32[]{:S(2)}) async-start(), calls=%async_computation.14 | async-start | bytes 2211840 | tf_op jit(solution)/shard_map/all_gather | solution.py:348
  539.2 338.6 %all-reduce.14.cloned.1.call-start = ((), (), s32[]{:S(2)}) async-start(), calls=%async_computation.16 | async-start | bytes 3833856 | tf_op jit(solution)/shard_map/psum | solution.py:349
  540.4 250.4 %copy-start.37 = (f32[512,768]{1,0:T(8,128)S(1)}, f32[512,768]{1,0:T(8,128)}, u32[]{:S(2)}) copy-start(f32[512,768]{1,0:T(8,128)} %copy-done.36) | copy-start | bytes 4718596
  790.8 4.9 copy-start.28
  790.8 4.9 copy-start.43
  790.8 4.9 copy-start.45
  790.8 4.9 copy-start.54
  (43 other events, 101.2 us)
Sparse Core Ops, SparseCore 0:
  9.9 36.8 all-gather.7
  48.7 24.0 all-gather.9
  74.6 38.9 all-gather.11
  115.3 38.9 all-gather.13
  156.1 38.8 all-gather.15
  491.0 48.0 reduce-scatter.15
  543.0 36.7 reduce-scatter.7
  583.6 53.8 reduce-scatter.13
  641.0 53.8 reduce-scatter.11
  698.5 53.8 reduce-scatter.9
  754.1 40.5 all-gather.17
  797.1 80.5 all-reduce.13
